TPU v7x, 512 devices: a whole 4x4x16 slice. The times are simulated.
512 devices in a mesh: seq: 128 (over x_hi, y, z), dp: 4 (over x_lo, core).
Axes of the slice: x: 4 (x_hi: 2, x_lo: 2; x = x_hi * 2 + x_lo), y: 4, z: 16, core: 2. Of those that a mesh axis runs over, the one named last changes fastest.
Arguments:
- asking_vectors: bfloat16 [4, 16384, 2048], P('dp', 'seq'), may hold values from -100 to 100
- lookup_vectors: bfloat16 [4, 16384, 2048], P('dp', 'seq'), may hold values from -13 to 13
- payload_vectors: bfloat16 [4, 16384, 2048], P('dp', 'seq'), may hold values from -6 to 6
- incoming_sensitivity: bfloat16 [4, 16384, 2048], P('dp', 'seq'), may hold values from -6 to 6
- learned_sharpness: float32 [16], replicated, may hold values from 0.5 to 2
- reply_list_sizes: int32 [4, 8], P('dp'), may hold values from 1 to 8192, 16384 in all within a row
Outputs:
- attention_result: bfloat16 [4, 16384, 2048], P('dp', 'seq')
- query_gradient: bfloat16 [4, 16384, 2048], P('dp', 'seq')
- key_gradient: bfloat16 [4, 16384, 2048], P('dp', 'seq')
- value_gradient: bfloat16 [4, 16384, 2048], P('dp', 'seq')
- scale_gradient: float32 [16], replicated
All inputs are finite; a program needn't handle non-finite values.
Results may differ from a plain program's by a relative error of at most 0.02.
The roundings to bfloat16 on the way count: a program that leaves them out, or rounds other values in their place, can miss the bound.
Values may be sent and summed in bfloat16 or wider, within the bound.
No kernel may reach another device: no remote copies, remote signals or barrier semaphores. Data moves between devices by JAX's collectives and lax.ppermute only.
A program may use at most 64 MiB of HBM per device.

v0:
```python
import math
import jax
import jax.numpy as jnp
from jax import lax
from jax.sharding import PartitionSpec as P

MIXER_CHANNELS = 16


def partner(array, axis, apart):
    return lax.ppermute(array, axis, [(i, i ^ 1 << apart) for i in range(lax.axis_size(axis))])


def level_plan(level_idx, head_idx, seq_devices):
    group_span = min(2**level_idx, seq_devices)
    dilation = max(1, group_span // 4)
    offset = (5 + head_idx * (dilation // 2)) % dilation
    return (group_span, dilation, offset)


def body(
    asking_vectors,
    lookup_vectors,
    payload_vectors,
    incoming_sensitivity,
    learned_sharpness,
    reply_list_sizes,
):
    seq_devices = lax.axis_size("seq")
    device_idx = lax.axis_index("seq")
    tokens = asking_vectors.shape[1]
    channel_extent = asking_vectors.shape[2] // MIXER_CHANNELS
    level_count = MIXER_CHANNELS // 2
    queries = asking_vectors[0]
    keyed = lookup_vectors[0]
    valued = payload_vectors[0]
    upstream = incoming_sensitivity[0]
    doc_ends = jnp.cumsum(reply_list_sizes[0])[:-1]

    def doc_of(positions):
        return jnp.sum((positions[..., None] >= doc_ends).astype(jnp.int32), axis=-1)

    def select_rows(source, channel_count, dilation, offset):
        column = channel_count * channel_extent
        column_block = source[:, column : column + channel_extent]
        return column_block.reshape(tokens // dilation, dilation, channel_extent)[:, offset]

    def spread_rows(values_sel, dilation, offset):
        per_dev = tokens // dilation
        holder = jnp.zeros((per_dev, dilation, channel_extent), values_sel.dtype)
        return holder.at[:, offset].set(values_sel).reshape(tokens, channel_extent)

    top_span = min(2 ** (level_count - 1), seq_devices)
    bit_order = list(range(top_span.bit_length() - 1))
    gathered, level_bits, level_masks = ([], [], [])
    for level_idx in range(level_count):
        group_span, dilation, offset_zero = level_plan(level_idx, 0, seq_devices)
        nbits = group_span.bit_length() - 1
        own_bits = [bit_num for bit_num in bit_order if bit_num < nbits]
        masks_now = [0]
        for bit_num in own_bits:
            masks_now = masks_now + [entry ^ 1 << bit_num for entry in masks_now]
        level_bits.append(own_bits)
        level_masks.append(masks_now)
        key_heads, val_heads = ([], [])
        for head_idx in range(2):
            offset = level_plan(level_idx, head_idx, seq_devices)[2]
            key_heads.append(select_rows(keyed, 2 * level_idx + head_idx, dilation, offset))
            val_heads.append(select_rows(valued, 2 * level_idx + head_idx, dilation, offset))
        gathered.append(
            jnp.concatenate([jnp.concatenate(key_heads, 1), jnp.concatenate(val_heads, 1)], 0)
        )
    for level_id in range(level_count):
        for bit_num in level_bits[level_id]:
            current = gathered[level_id]
            gathered[level_id] = jnp.concatenate([current, partner(current, "seq", bit_num)], 0)
    out_cols, dq_cols, scale_terms, level_grads = ([], [], [], [])
    for level_id in range(level_count):
        group_span, dilation, offset_zero = level_plan(level_id, 0, seq_devices)
        per_dev = tokens // dilation
        arranged = gathered[level_id].reshape(group_span, 2, per_dev, 2 * channel_extent)
        all_keys = arranged[:, 0].reshape(group_span * per_dev, 2 * channel_extent)
        all_vals = arranged[:, 1].reshape(group_span * per_dev, 2 * channel_extent)
        sources = jnp.bitwise_xor(device_idx, jnp.array(level_masks[level_id], jnp.int32))
        key_grad_heads, val_grad_heads = ([], [])
        for head_idx in range(2):
            offset = level_plan(level_id, head_idx, seq_devices)[2]
            channel_count = 2 * level_id + head_idx
            local_idx = jnp.arange(per_dev, dtype=jnp.int32) * dilation + offset
            query_docs = doc_of(device_idx * tokens + local_idx)
            key_docs = doc_of((sources[:, None] * tokens + local_idx[None, :]).reshape(-1))
            allowed = query_docs[:, None] == key_docs[None, :]
            query_sel = select_rows(queries, channel_count, dilation, offset)
            up_sel = select_rows(upstream, channel_count, dilation, offset)
            key_sel = all_keys[:, head_idx * channel_extent : (head_idx + 1) * channel_extent]
            val_sel = all_vals[:, head_idx * channel_extent : (head_idx + 1) * channel_extent]
            raw = lax.dot_general(
                query_sel, key_sel, (((1,), (1,)), ((), ())), preferred_element_type=jnp.float32
            )
            logit_multiplier = learned_sharpness[channel_count] / math.sqrt(channel_extent)
            scores = jnp.where(allowed, raw * logit_multiplier, -jnp.inf)
            highest = jnp.max(scores, axis=1, keepdims=True)
            expo = jnp.where(allowed, jnp.exp(scores - highest), 0.0)
            probs = expo / jnp.sum(expo, axis=1, keepdims=True)
            probs_narrow = probs.astype(jnp.bfloat16)
            attended_output = jnp.dot(probs_narrow, val_sel, preferred_element_type=jnp.float32)
            delta = jnp.sum(up_sel.astype(jnp.float32) * attended_output, axis=1, keepdims=True)
            gradient_probs = lax.dot_general(
                up_sel, val_sel, (((1,), (1,)), ((), ())), preferred_element_type=jnp.float32
            )
            dscores = probs * (gradient_probs - delta)
            scale_terms.append(jnp.sum(dscores * raw) / math.sqrt(channel_extent))
            dscore_low = dscores.astype(jnp.bfloat16)
            grad_q = (
                jnp.dot(dscore_low, key_sel, preferred_element_type=jnp.float32) * logit_multiplier
            )
            grad_k = (
                lax.dot_general(
                    dscore_low,
                    query_sel,
                    (((0,), (0,)), ((), ())),
                    preferred_element_type=jnp.float32,
                )
                * logit_multiplier
            )
            grad_v = lax.dot_general(
                probs_narrow, up_sel, (((0,), (0,)), ((), ())), preferred_element_type=jnp.float32
            )
            out_cols.append(spread_rows(attended_output.astype(jnp.bfloat16), dilation, offset))
            dq_cols.append(spread_rows(grad_q.astype(jnp.bfloat16), dilation, offset))
            key_grad_heads.append(grad_k)
            val_grad_heads.append(grad_v)
        key_pack = jnp.concatenate(key_grad_heads, 1).reshape(
            group_span, per_dev, 2 * channel_extent
        )
        val_pack = jnp.concatenate(val_grad_heads, 1).reshape(
            group_span, per_dev, 2 * channel_extent
        )
        level_grads.append(
            jnp.stack([key_pack, val_pack], 1).reshape(group_span * 2 * per_dev, 2 * channel_extent)
        )
    for level_id in range(level_count):
        for bit_num in level_bits[level_id][::-1]:
            current = level_grads[level_id]
            half_rows = current.shape[0] // 2
            level_grads[level_id] = current[:half_rows] + partner(
                current[half_rows:], "seq", bit_num
            )
    dk_cols, dv_cols = ([], [])
    for level_id in range(level_count):
        group_span, dilation, offset_zero = level_plan(level_id, 0, seq_devices)
        per_dev = tokens // dilation
        own_grad = level_grads[level_id]
        for head_idx in range(2):
            offset = level_plan(level_id, head_idx, seq_devices)[2]
            cols_lo = head_idx * channel_extent
            key_part = own_grad[:per_dev, cols_lo : cols_lo + channel_extent]
            val_part = own_grad[per_dev:, cols_lo : cols_lo + channel_extent]
            dk_cols.append(spread_rows(key_part.astype(jnp.bfloat16), dilation, offset))
            dv_cols.append(spread_rows(val_part.astype(jnp.bfloat16), dilation, offset))
    scale_gradient = lax.psum(jnp.stack(scale_terms), ("seq", "dp"))
    attention_result = jnp.concatenate(out_cols, 1)[None]
    query_gradient = jnp.concatenate(dq_cols, 1)[None]
    key_gradient = jnp.concatenate(dk_cols, 1)[None]
    value_gradient = jnp.concatenate(dv_cols, 1)[None]
    return (attention_result, query_gradient, key_gradient, value_gradient, scale_gradient)


def solution(mesh):
    in_specs = (
        P("dp", "seq", None),
        P("dp", "seq", None),
        P("dp", "seq", None),
        P("dp", "seq", None),
        P(),
        P("dp", None),
    )
    out_specs = (
        P("dp", "seq", None),
        P("dp", "seq", None),
        P("dp", "seq", None),
        P("dp", "seq", None),
        P(),
    )
    return jax.shard_map(body, mesh=mesh, in_specs=in_specs, out_specs=out_specs, check_vma=False)
```

profile of v0, /device:TPU:4, one launch (start us, length us, event | category | flops | bytes accessed | tf_op | source)
XLA Modules:
  0.0 628.4 jit_solution(6130555929108911474)
XLA Ops:
  2.0 3.8 collective-permute-start.21
  8.1 3.8 collective-permute-start.10
  14.2 3.8 collective-permute-start.3
  61.6 5.2 collective-permute-start.22
  68.4 3.8 collective-permute-start
  72.2 4.8 collective-permute-start.16
  78.7 9.1 %collective-permute-start.23 = (bf16[32,256]{1,0:T(8,128)(2,1)S(1)}, bf16[32,256]{1,0:T(8,128)(2,1)S(1)}, u32[]{:S(2)}, u32[]{:S(2)}) collective-permute-start(bf16[32,256]{1,0:T(8,128)(2,1)S(1)} %pad_maximum_fusion.36), channel_id=1, source_target_pairs={{0,16},{4,20},{8,24},{12,28},{16,0},{20,4},{24,8},{28,12},{32,48},... | collective-permute-start | bytes 49160 | tf_op jit(solution)/shard_map/ppermute | solution.py:11
  89.5 4.8 collective-permute-start.11
  94.4 7.8 %collective-permute-start.17 = (bf16[64,256]{1,0:T(8,128)(2,1)S(1)}, bf16[64,256]{1,0:T(8,128)(2,1)S(1)}, u32[]{:S(2)}, u32[]{:S(2)}) collective-permute-start(bf16[64,256]{1,0:T(8,128)(2,1)S(1)} %pad_maximum_fusion.32), channel_id=1, source_target_pairs={{0,16},{4,20},{8,24},{12,28},{16,0},{20,4},{24,8},{28,12},{32,48},... | collective-permute-start | bytes 98312 | tf_op jit(solution)/shard_map/ppermute | solution.py:11
  102.9 8.2 %collective-permute-start.24 = (bf16[64,256]{1,0:T(8,128)(2,1)S(1)}, bf16[64,256]{1,0:T(8,128)(2,1)S(1)}, u32[]{:S(2)}, u32[]{:S(2)}) collective-permute-start(bf16[64,256]{1,0:T(8,128)(2,1)S(1)} %concatenate.419), channel_id=1, source_target_pairs={{0,32},{4,36},{8,40},{12,44},{16,48},{20,52},{24,56},{28,60},{32,0... | collective-permute-start | bytes 98312 | tf_op jit(solution)/shard_map/ppermute | solution.py:11
  111.7 3.4 collective-permute-start.7
  117.5 3.7 collective-permute-start.12
  121.3 10.2 %collective-permute-start.18 = (bf16[128,256]{1,0:T(8,128)(2,1)}, bf16[128,256]{1,0:T(8,128)(2,1)S(1)}, u32[]{:S(2)}, u32[]{:S(2)}) collective-permute-start(bf16[128,256]{1,0:T(8,128)(2,1)} %get-tuple-element.952), channel_id=1, source_target_pairs={{0,32},{4,36},{8,40},{12,44},{16,48},{20,52},{24,56},{28,60},{32,0... | collective-permute-start | bytes 196616 | tf_op jit(solution)/shard_map/ppermute | solution.py:11
  132.1 3.5 collective-permute-start.25
  136.9 3.1 collective-permute-start.4
  140.7 4.2 collective-permute-start.8
  145.6 6.4 %collective-permute-start.13 = (bf16[256,256]{1,0:T(8,128)(2,1)}, bf16[256,256]{1,0:T(8,128)(2,1)}, u32[]{:S(2)}, u32[]{:S(2)}) collective-permute-start(bf16[256,256]{1,0:T(8,128)(2,1)} %get-tuple-element.938), channel_id=1, source_target_pairs={{0,32},{4,36},{8,40},{12,44},{16,48},{20,52},{24,56},{28,60},{32,0... | collective-permute-start | bytes 393224 | tf_op jit(solution)/shard_map/ppermute | solution.py:11
  152.0 3.6 concatenate.421
  155.7 3.1 collective-permute-start.19
  163.4 5.0 collective-permute-start.26
  168.5 2.8 collective-permute-start.2
  172.1 6.6 %collective-permute-start.5 = (bf16[512,256]{1,0:T(8,128)(2,1)}, bf16[512,256]{1,0:T(8,128)(2,1)}, u32[]{:S(2)}, u32[]{:S(2)}) collective-permute-start(bf16[512,256]{1,0:T(8,128)(2,1)} %pad_maximum_fusion.21), channel_id=1, source_target_pairs={{0,16},{4,20},{8,24},{12,28},{16,0},{20,4},{24,8},{28,12},{32,48},... | collective-permute-start | bytes 786440 | tf_op jit(solution)/shard_map/ppermute | solution.py:11
  180.3 7.2 %collective-permute-start.9 = (bf16[512,256]{1,0:T(8,128)(2,1)}, bf16[512,256]{1,0:T(8,128)(2,1)}, u32[]{:S(2)}, u32[]{:S(2)}) collective-permute-start(bf16[512,256]{1,0:T(8,128)(2,1)} %get-tuple-element.925), channel_id=1, source_target_pairs={{0,32},{4,36},{8,40},{12,44},{16,48},{20,52},{24,56},{28,60},{32,0... | collective-permute-start | bytes 786440 | tf_op jit(solution)/shard_map/ppermute | solution.py:11
  193.4 3.7 collective-permute-start.20
  197.1 4.3 concatenate.422
  202.1 3.1 collective-permute-start.27
  277.4 7.0 %collective-permute-start.31 = (f32[512,256]{1,0:T(8,128)}, f32[512,256]{1,0:T(8,128)}, u32[]{:S(2)}, u32[]{:S(2)}) collective-permute-start(f32[512,256]{1,0:T(8,128)} %bitcast.190), channel_id=1, source_target_pairs={{0,16},{4,20},{8,24},{12,28},{16,0},{20,4},{24,8},{28,12},{32,48},... | collective-permute-start | bytes 1572872 | tf_op jit(solution)/shard_map/ppermute | solution.py:11
  305.9 6.2 collective-permute-start.34
  336.0 4.0 collective-permute-start.38
  368.8 98.5 %psum.7 = f32[16]{0:T(128)} all-reduce(f32[16]{0:T(128)S(1)} %stack.99), channel_id=1, replica_groups=mesh['seq'=128,'dp'=4] {'seq','dp'}, use_global_device_ids=true, to_apply=%region_89.90 | all-reduce | flops 16 | bytes 128 | tf_op jit(solution)/shard_map/psum | solution.py:161
  476.6 3.1 collective-permute-start.43
  481.3 4.4 collective-permute-start.49
  486.9 4.0 collective-permute-start.30
  495.3 6.1 collective-permute-start.35
  502.5 6.6 %collective-permute-start.39 = (f32[256,256]{1,0:T(8,128)S(1)}, f32[256,256]{1,0:T(8,128)S(1)}, u32[]{:S(2)}, u32[]{:S(2)}) collective-permute-start(f32[256,256]{1,0:T(8,128)S(1)} %slice.2481), channel_id=1, source_target_pairs={{0,32},{4,36},{8,40},{12,44},{16,48},{20,52},{24,56},{28,60},{32,0... | collective-permute-start | bytes 786440 | tf_op jit(solution)/shard_map/ppermute | solution.py:11
  509.3 3.4 collective-permute-start.44
  512.8 4.0 collective-permute-start.50
  517.5 8.3 %collective-permute-done.32 = f32[256,256]{1,0:T(8,128)S(1)} collective-permute-done((f32[256,256]{1,0:T(8,128)S(1)}, f32[256,256]{1,0:T(8,128)S(1)}, u32[]{:S(2)}, u32[]{:S(2)}) %collective-permute-start.32) | collective-permute-done | bytes 262176 | tf_op jit(solution)/shard_map/ppermute | solution.py:11
  527.8 19.5 %collective-permute-done.35 = f32[256,256]{1,0:T(8,128)S(1)} collective-permute-done((f32[256,256]{1,0:T(8,128)S(1)}, f32[256,256]{1,0:T(8,128)S(1)}, u32[]{:S(2)}, u32[]{:S(2)}) %collective-permute-start.35) | collective-permute-done | bytes 262176 | tf_op jit(solution)/shard_map/ppermute | solution.py:11
  551.4 7.9 %collective-permute-start.45 = (f32[128,256]{1,0:T(8,128)S(1)}, f32[128,256]{1,0:T(8,128)S(1)}, u32[]{:S(2)}, u32[]{:S(2)}) collective-permute-start(f32[128,256]{1,0:T(8,128)S(1)} %slice.2495), channel_id=1, source_target_pairs={{0,32},{4,36},{8,40},{12,44},{16,48},{20,52},{24,56},{28,60},{32,0... | collective-permute-start | bytes 393224 | tf_op jit(solution)/shard_map/ppermute | solution.py:11
  562.5 7.4 %collective-permute-start.37 = (f32[64,256]{1,0:T(8,128)S(1)}, f32[64,256]{1,0:T(8,128)S(1)}, u32[]{:S(2)}, u32[]{:S(2)}) collective-permute-start(f32[64,256]{1,0:T(8,128)S(1)} %slice.2475), channel_id=1, source_target_pairs={{0,4},{4,0},{8,12},{12,8},{16,20},{20,16},{24,28},{28,24},{32,36},... | collective-permute-start | bytes 196616 | tf_op jit(solution)/shard_map/ppermute | solution.py:11
  569.9 5.5 collective-permute-done.40
  577.5 9.5 %collective-permute-start.46 = (f32[64,256]{1,0:T(8,128)S(1)}, f32[64,256]{1,0:T(8,128)S(1)}, u32[]{:S(2)}, u32[]{:S(2)}) collective-permute-start(f32[64,256]{1,0:T(8,128)S(1)} %slice.2497), channel_id=1, source_target_pairs={{0,16},{4,20},{8,24},{12,28},{16,0},{20,4},{24,8},{28,12},{32,48},... | collective-permute-start | bytes 196616 | tf_op jit(solution)/shard_map/ppermute | solution.py:11
  587.0 8.0 %collective-permute-start.52 = (f32[64,256]{1,0:T(8,128)S(1)}, f32[64,256]{1,0:T(8,128)S(1)}, u32[]{:S(2)}, u32[]{:S(2)}) collective-permute-start(f32[64,256]{1,0:T(8,128)S(1)} %slice.2511), channel_id=1, source_target_pairs={{0,32},{4,36},{8,40},{12,44},{16,48},{20,52},{24,56},{28,60},{32,0... | collective-permute-start | bytes 196616 | tf_op jit(solution)/shard_map/ppermute | solution.py:11
  599.7 4.2 collective-permute-done.52
  609.2 4.4 collective-permute-done.53
  616.3 3.9 collective-permute-done.54
  622.2 3.6 collective-permute-done.55
  (863 shorter events, 245.0 us)
Async XLA Ops:
  2.0 57.5 %collective-permute-start.21 = (bf16[8,256]{1,0:T(8,128)(2,1)S(1)}, bf16[8,256]{1,0:T(8,128)(2,1)S(1)}, u32[]{:S(2)}, u32[]{:S(2)}) collective-permute-start(bf16[8,256]{1,0:T(8,128)(2,1)S(1)} %maximum_maximum_fusion.4), channel_id=1, source_target_pairs={{0,4},{4,0},{8,12},{12,8},{16,20},{20,16},{24,28},{28,24},{32,36},... | collective-permute-start | bytes 12296 | tf_op jit(solution)/shard_map/ppermute | solution.py:11
  5.9 55.6 %collective-permute-start.15 = (bf16[16,256]{1,0:T(8,128)(2,1)S(1)}, bf16[16,256]{1,0:T(8,128)(2,1)S(1)}, u32[]{:S(2)}, u32[]{:S(2)}) collective-permute-start(bf16[16,256]{1,0:T(8,128)(2,1)S(1)} %maximum_maximum_fusion.3), channel_id=1, source_target_pairs={{0,4},{4,0},{8,12},{12,8},{16,20},{20,16},{24,28},{28,24},{32,36},... | collective-permute-start | bytes 24584 | tf_op jit(solution)/shard_map/ppermute | solution.py:11
  8.1 64.1 %collective-permute-start.10 = (bf16[32,256]{1,0:T(8,128)(2,1)S(1)}, bf16[32,256]{1,0:T(8,128)(2,1)S(1)}, u32[]{:S(2)}, u32[]{:S(2)}) collective-permute-start(bf16[32,256]{1,0:T(8,128)(2,1)S(1)} %maximum_maximum_fusion.2), channel_id=1, source_target_pairs={{0,4},{4,0},{8,12},{12,8},{16,20},{20,16},{24,28},{28,24},{32,36},... | collective-permute-start | bytes 49160 | tf_op jit(solution)/shard_map/ppermute | solution.py:11
  12.1 82.3 %collective-permute-start.6 = (bf16[64,256]{1,0:T(8,128)(2,1)S(1)}, bf16[64,256]{1,0:T(8,128)(2,1)S(1)}, u32[]{:S(2)}, u32[]{:S(2)}) collective-permute-start(bf16[64,256]{1,0:T(8,128)(2,1)S(1)} %maximum_maximum_fusion.1), channel_id=1, source_target_pairs={{0,4},{4,0},{8,12},{12,8},{16,20},{20,16},{24,28},{28,24},{32,36},... | collective-permute-start | bytes 98312 | tf_op jit(solution)/shard_map/ppermute | solution.py:11
  14.2 107.0 %collective-permute-start.3 = (bf16[128,256]{1,0:T(8,128)(2,1)S(1)}, bf16[128,256]{1,0:T(8,128)(2,1)S(1)}, u32[]{:S(2)}, u32[]{:S(2)}) collective-permute-start(bf16[128,256]{1,0:T(8,128)(2,1)S(1)} %maximum_maximum_fusion), channel_id=1, source_target_pairs={{0,4},{4,0},{8,12},{12,8},{16,20},{20,16},{24,28},{28,24},{32,36},... | collective-permute-start | bytes 196616 | tf_op jit(solution)/shard_map/ppermute | solution.py:11
  59.5 103.3 %collective-permute-start.1 = (bf16[256,256]{1,0:T(8,128)(2,1)S(1)}, bf16[256,256]{1,0:T(8,128)(2,1)S(1)}, u32[]{:S(2)}, u32[]{:S(2)}) collective-permute-start(bf16[256,256]{1,0:T(8,128)(2,1)S(1)} %pad_maximum_fusion.26), channel_id=1, source_target_pairs={{0,4},{4,0},{8,12},{12,8},{16,20},{20,16},{24,28},{28,24},{32,36},... | collective-permute-start | bytes 393224 | tf_op jit(solution)/shard_map/ppermute | solution.py:11
  68.4 87.3 %collective-permute-start = (bf16[256,256]{1,0:T(8,128)(2,1)S(1)}, bf16[256,256]{1,0:T(8,128)(2,1)S(1)}, u32[]{:S(2)}, u32[]{:S(2)}) collective-permute-start(bf16[256,256]{1,0:T(8,128)(2,1)S(1)} %pad_maximum_fusion.25), channel_id=1, source_target_pairs={{0,4},{4,0},{8,12},{12,8},{16,20},{20,16},{24,28},{28,24},{32,36},... | collective-permute-start | bytes 393224 | tf_op jit(solution)/shard_map/ppermute | solution.py:11
  78.7 10.8 %collective-permute-start.23 = (bf16[32,256]{1,0:T(8,128)(2,1)S(1)}, bf16[32,256]{1,0:T(8,128)(2,1)S(1)}, u32[]{:S(2)}, u32[]{:S(2)}) collective-permute-start(bf16[32,256]{1,0:T(8,128)(2,1)S(1)} %pad_maximum_fusion.36), channel_id=1, source_target_pairs={{0,16},{4,20},{8,24},{12,28},{16,0},{20,4},{24,8},{28,12},{32,48},... | collective-permute-start | bytes 49160 | tf_op jit(solution)/shard_map/ppermute | solution.py:11
  89.5 13.3 %collective-permute-start.11 = (bf16[64,256]{1,0:T(8,128)(2,1)S(1)}, bf16[64,256]{1,0:T(8,128)(2,1)S(1)}, u32[]{:S(2)}, u32[]{:S(2)}) collective-permute-start(bf16[64,256]{1,0:T(8,128)(2,1)S(1)} %pad_maximum_fusion.31), channel_id=1, source_target_pairs={{0,8},{4,12},{8,0},{12,4},{16,24},{20,28},{24,16},{28,20},{32,40},... | collective-permute-start | bytes 98312 | tf_op jit(solution)/shard_map/ppermute | solution.py:11
  94.4 17.4 %collective-permute-start.17 = (bf16[64,256]{1,0:T(8,128)(2,1)S(1)}, bf16[64,256]{1,0:T(8,128)(2,1)S(1)}, u32[]{:S(2)}, u32[]{:S(2)}) collective-permute-start(bf16[64,256]{1,0:T(8,128)(2,1)S(1)} %pad_maximum_fusion.32), channel_id=1, source_target_pairs={{0,16},{4,20},{8,24},{12,28},{16,0},{20,4},{24,8},{28,12},{32,48},... | collective-permute-start | bytes 98312 | tf_op jit(solution)/shard_map/ppermute | solution.py:11
  102.9 14.6 %collective-permute-start.24 = (bf16[64,256]{1,0:T(8,128)(2,1)S(1)}, bf16[64,256]{1,0:T(8,128)(2,1)S(1)}, u32[]{:S(2)}, u32[]{:S(2)}) collective-permute-start(bf16[64,256]{1,0:T(8,128)(2,1)S(1)} %concatenate.419), channel_id=1, source_target_pairs={{0,32},{4,36},{8,40},{12,44},{16,48},{20,52},{24,56},{28,60},{32,0... | collective-permute-start | bytes 98312 | tf_op jit(solution)/shard_map/ppermute | solution.py:11
  111.7 20.4 %collective-permute-start.7 = (bf16[128,256]{1,0:T(8,128)(2,1)S(1)}, bf16[128,256]{1,0:T(8,128)(2,1)S(1)}, u32[]{:S(2)}, u32[]{:S(2)}) collective-permute-start(bf16[128,256]{1,0:T(8,128)(2,1)S(1)} %pad_maximum_fusion.29), channel_id=1, source_target_pairs={{0,8},{4,12},{8,0},{12,4},{16,24},{20,28},{24,16},{28,20},{32,40},... | collective-permute-start | bytes 196616 | tf_op jit(solution)/shard_map/ppermute | solution.py:11
  117.5 19.4 %collective-permute-start.12 = (bf16[128,256]{1,0:T(8,128)(2,1)S(1)}, bf16[128,256]{1,0:T(8,128)(2,1)S(1)}, u32[]{:S(2)}, u32[]{:S(2)}) collective-permute-start(bf16[128,256]{1,0:T(8,128)(2,1)S(1)} %pad_maximum_fusion.30), channel_id=1, source_target_pairs={{0,16},{4,20},{8,24},{12,28},{16,0},{20,4},{24,8},{28,12},{32,48},... | collective-permute-start | bytes 196616 | tf_op jit(solution)/shard_map/ppermute | solution.py:11
  121.3 19.5 %collective-permute-start.18 = (bf16[128,256]{1,0:T(8,128)(2,1)}, bf16[128,256]{1,0:T(8,128)(2,1)S(1)}, u32[]{:S(2)}, u32[]{:S(2)}) collective-permute-start(bf16[128,256]{1,0:T(8,128)(2,1)} %get-tuple-element.952), channel_id=1, source_target_pairs={{0,32},{4,36},{8,40},{12,44},{16,48},{20,52},{24,56},{28,60},{32,0... | collective-permute-start | bytes 196616 | tf_op jit(solution)/shard_map/ppermute | solution.py:11
  132.1 13.5 %collective-permute-start.25 = (bf16[128,256]{1,0:T(8,128)(2,1)S(1)}, bf16[128,256]{1,0:T(8,128)(2,1)S(1)}, u32[]{:S(2)}, u32[]{:S(2)}) collective-permute-start(bf16[128,256]{1,0:T(8,128)(2,1)S(1)} %concatenate.420), channel_id=1, source_target_pairs={{0,64},{4,68},{8,72},{12,76},{16,80},{20,84},{24,88},{28,92},{32,9... | collective-permute-start | bytes 196616 | tf_op jit(solution)/shard_map/ppermute | solution.py:11
  136.9 31.5 %collective-permute-start.4 = (bf16[256,256]{1,0:T(8,128)(2,1)}, bf16[256,256]{1,0:T(8,128)(2,1)S(1)}, u32[]{:S(2)}, u32[]{:S(2)}) collective-permute-start(bf16[256,256]{1,0:T(8,128)(2,1)} %pad_maximum_fusion.27), channel_id=1, source_target_pairs={{0,8},{4,12},{8,0},{12,4},{16,24},{20,28},{24,16},{28,20},{32,40},... | collective-permute-start | bytes 393224 | tf_op jit(solution)/shard_map/ppermute | solution.py:11
  140.7 31.3 %collective-permute-start.8 = (bf16[256,256]{1,0:T(8,128)(2,1)}, bf16[256,256]{1,0:T(8,128)(2,1)}, u32[]{:S(2)}, u32[]{:S(2)}) collective-permute-start(bf16[256,256]{1,0:T(8,128)(2,1)} %pad_maximum_fusion.28), channel_id=1, source_target_pairs={{0,16},{4,20},{8,24},{12,28},{16,0},{20,4},{24,8},{28,12},{32,48},... | collective-permute-start | bytes 393224 | tf_op jit(solution)/shard_map/ppermute | solution.py:11
  145.6 34.8 %collective-permute-start.13 = (bf16[256,256]{1,0:T(8,128)(2,1)}, bf16[256,256]{1,0:T(8,128)(2,1)}, u32[]{:S(2)}, u32[]{:S(2)}) collective-permute-start(bf16[256,256]{1,0:T(8,128)(2,1)} %get-tuple-element.938), channel_id=1, source_target_pairs={{0,32},{4,36},{8,40},{12,44},{16,48},{20,52},{24,56},{28,60},{32,0... | collective-permute-start | bytes 393224 | tf_op jit(solution)/shard_map/ppermute | solution.py:11
  155.7 33.5 %collective-permute-start.19 = (bf16[256,256]{1,0:T(8,128)(2,1)}, bf16[256,256]{1,0:T(8,128)(2,1)}, u32[]{:S(2)}, u32[]{:S(2)}) collective-permute-start(bf16[256,256]{1,0:T(8,128)(2,1)} %get-tuple-element.935), channel_id=1, source_target_pairs={{0,64},{4,68},{8,72},{12,76},{16,80},{20,84},{24,88},{28,92},{32,9... | collective-permute-start | bytes 393224 | tf_op jit(solution)/shard_map/ppermute | solution.py:11
  163.4 30.0 %collective-permute-start.26 = (bf16[256,256]{1,0:T(8,128)(2,1)S(1)}, bf16[256,256]{1,0:T(8,128)(2,1)S(1)}, u32[]{:S(2)}, u32[]{:S(2)}) collective-permute-start(bf16[256,256]{1,0:T(8,128)(2,1)S(1)} %copy-done.25), channel_id=1, source_target_pairs={{0,128},{4,132},{8,136},{12,140},{16,144},{20,148},{24,152},{28,15... | collective-permute-start | bytes 393224 | tf_op jit(solution)/shard_map/ppermute | solution.py:11
  168.5 33.0 %collective-permute-start.2 = (bf16[512,256]{1,0:T(8,128)(2,1)S(1)}, bf16[512,256]{1,0:T(8,128)(2,1)S(1)}, u32[]{:S(2)}, u32[]{:S(2)}) collective-permute-start(bf16[512,256]{1,0:T(8,128)(2,1)S(1)} %pad_maximum_fusion.20), channel_id=1, source_target_pairs={{0,8},{4,12},{8,0},{12,4},{16,24},{20,28},{24,16},{28,20},{32,40},... | collective-permute-start | bytes 786440 | tf_op jit(solution)/shard_map/ppermute | solution.py:11
  172.1 65.1 %collective-permute-start.5 = (bf16[512,256]{1,0:T(8,128)(2,1)}, bf16[512,256]{1,0:T(8,128)(2,1)}, u32[]{:S(2)}, u32[]{:S(2)}) collective-permute-start(bf16[512,256]{1,0:T(8,128)(2,1)} %pad_maximum_fusion.21), channel_id=1, source_target_pairs={{0,16},{4,20},{8,24},{12,28},{16,0},{20,4},{24,8},{28,12},{32,48},... | collective-permute-start | bytes 786440 | tf_op jit(solution)/shard_map/ppermute | solution.py:11
  180.3 73.6 %collective-permute-start.9 = (bf16[512,256]{1,0:T(8,128)(2,1)}, bf16[512,256]{1,0:T(8,128)(2,1)}, u32[]{:S(2)}, u32[]{:S(2)}) collective-permute-start(bf16[512,256]{1,0:T(8,128)(2,1)} %get-tuple-element.925), channel_id=1, source_target_pairs={{0,32},{4,36},{8,40},{12,44},{16,48},{20,52},{24,56},{28,60},{32,0... | collective-permute-start | bytes 786440 | tf_op jit(solution)/shard_map/ppermute | solution.py:11
  189.2 88.2 %collective-permute-start.14 = (bf16[512,256]{1,0:T(8,128)(2,1)}, bf16[512,256]{1,0:T(8,128)(2,1)}, u32[]{:S(2)}, u32[]{:S(2)}) collective-permute-start(bf16[512,256]{1,0:T(8,128)(2,1)} %get-tuple-element.923), channel_id=1, source_target_pairs={{0,64},{4,68},{8,72},{12,76},{16,80},{20,84},{24,88},{28,92},{32,9... | collective-permute-start | bytes 786440 | tf_op jit(solution)/shard_map/ppermute | solution.py:11
  193.4 112.5 %collective-permute-start.20 = (bf16[512,256]{1,0:T(8,128)(2,1)}, bf16[512,256]{1,0:T(8,128)(2,1)}, u32[]{:S(2)}, u32[]{:S(2)}) collective-permute-start(bf16[512,256]{1,0:T(8,128)(2,1)} %get-tuple-element.921), channel_id=1, source_target_pairs={{0,128},{4,132},{8,136},{12,140},{16,144},{20,148},{24,152},{28,15... | collective-permute-start | bytes 786440 | tf_op jit(solution)/shard_map/ppermute | solution.py:11
  202.1 133.9 %collective-permute-start.27 = (bf16[512,256]{1,0:T(8,128)(2,1)}, bf16[512,256]{1,0:T(8,128)(2,1)}, u32[]{:S(2)}, u32[]{:S(2)}) collective-permute-start(bf16[512,256]{1,0:T(8,128)(2,1)} %concatenate.422), channel_id=1, source_target_pairs={{0,256},{4,260},{8,264},{12,268},{16,272},{20,276},{24,280},{28,28... | collective-permute-start | bytes 786440 | tf_op jit(solution)/shard_map/ppermute | solution.py:11
  237.2 244.1 %collective-permute-start.29 = (f32[512,256]{0,1:T(8,128)}, f32[512,256]{0,1:T(8,128)}, u32[]{:S(2)}, u32[]{:S(2)}) collective-permute-start(f32[512,256]{0,1:T(8,128)} %slice.2212), channel_id=1, source_target_pairs={{0,8},{4,12},{8,0},{12,4},{16,24},{20,28},{24,16},{28,20},{32,40},... | collective-permute-start | bytes 1572872 | tf_op jit(solution)/shard_map/ppermute | solution.py:11
  253.9 222.6 %collective-permute-start.28 = (f32[256,256]{0,1:T(8,128)}, f32[256,256]{0,1:T(8,128)}, u32[]{:S(2)}, u32[]{:S(2)}) collective-permute-start(f32[256,256]{0,1:T(8,128)} %bitcast.622), channel_id=1, source_target_pairs={{0,4},{4,0},{8,12},{12,8},{16,20},{20,16},{24,28},{28,24},{32,36},... | collective-permute-start | bytes 786440 | tf_op jit(solution)/shard_map/ppermute | solution.py:11
  277.4 209.5 %collective-permute-start.31 = (f32[512,256]{1,0:T(8,128)}, f32[512,256]{1,0:T(8,128)}, u32[]{:S(2)}, u32[]{:S(2)}) collective-permute-start(f32[512,256]{1,0:T(8,128)} %bitcast.190), channel_id=1, source_target_pairs={{0,16},{4,20},{8,24},{12,28},{16,0},{20,4},{24,8},{28,12},{32,48},... | collective-permute-start | bytes 1572872 | tf_op jit(solution)/shard_map/ppermute | solution.py:11
  305.9 186.0 %collective-permute-start.34 = (f32[512,256]{1,0:T(8,128)}, f32[512,256]{1,0:T(8,128)}, u32[]{:S(2)}, u32[]{:S(2)}) collective-permute-start(f32[512,256]{1,0:T(8,128)} %bitcast.198), channel_id=1, source_target_pairs={{0,32},{4,36},{8,40},{12,44},{16,48},{20,52},{24,56},{28,60},{32,0... | collective-permute-start | bytes 1572872 | tf_op jit(solution)/shard_map/ppermute | solution.py:11
  336.0 159.3 %collective-permute-start.38 = (f32[512,256]{1,0:T(8,128)}, f32[512,256]{1,0:T(8,128)}, u32[]{:S(2)}, u32[]{:S(2)}) collective-permute-start(f32[512,256]{1,0:T(8,128)} %bitcast.206), channel_id=1, source_target_pairs={{0,64},{4,68},{8,72},{12,76},{16,80},{20,84},{24,88},{28,92},{32,9... | collective-permute-start | bytes 1572872 | tf_op jit(solution)/shard_map/ppermute | solution.py:11
  476.6 26.0 %collective-permute-start.43 = (f32[512,256]{1,0:T(8,128)}, f32[512,256]{1,0:T(8,128)S(1)}, u32[]{:S(2)}, u32[]{:S(2)}) collective-permute-start(f32[512,256]{1,0:T(8,128)} %bitcast.691), channel_id=1, source_target_pairs={{0,128},{4,132},{8,136},{12,140},{16,144},{20,148},{24,152},{28,15... | collective-permute-start | bytes 1572872 | tf_op jit(solution)/shard_map/ppermute | solution.py:11
  481.3 28.0 %collective-permute-start.49 = (f32[512,256]{1,0:T(8,128)S(1)}, f32[512,256]{1,0:T(8,128)S(1)}, u32[]{:S(2)}, u32[]{:S(2)}) collective-permute-start(f32[512,256]{1,0:T(8,128)S(1)} %copy-done.8), channel_id=1, source_target_pairs={{0,256},{4,260},{8,264},{12,268},{16,272},{20,276},{24,280},{28,28... | collective-permute-start | bytes 1572872 | tf_op jit(solution)/shard_map/ppermute | solution.py:11
  486.9 25.9 %collective-permute-start.30 = (f32[256,256]{0,1:T(8,128)S(1)}, f32[256,256]{0,1:T(8,128)S(1)}, u32[]{:S(2)}, u32[]{:S(2)}) collective-permute-start(f32[256,256]{0,1:T(8,128)S(1)} %slice.2458), channel_id=1, source_target_pairs={{0,4},{4,0},{8,12},{12,8},{16,20},{20,16},{24,28},{28,24},{32,36},... | collective-permute-start | bytes 786440 | tf_op jit(solution)/shard_map/ppermute | solution.py:11
  492.0 33.9 %collective-permute-start.32 = (f32[256,256]{1,0:T(8,128)S(1)}, f32[256,256]{1,0:T(8,128)S(1)}, u32[]{:S(2)}, u32[]{:S(2)}) collective-permute-start(f32[256,256]{1,0:T(8,128)S(1)} %slice.2463), channel_id=1, source_target_pairs={{0,8},{4,12},{8,0},{12,4},{16,24},{20,28},{24,16},{28,20},{32,40},... | collective-permute-start | bytes 786440 | tf_op jit(solution)/shard_map/ppermute | solution.py:11
  495.3 52.0 %collective-permute-start.35 = (f32[256,256]{1,0:T(8,128)S(1)}, f32[256,256]{1,0:T(8,128)S(1)}, u32[]{:S(2)}, u32[]{:S(2)}) collective-permute-start(f32[256,256]{1,0:T(8,128)S(1)} %slice.2471), channel_id=1, source_target_pairs={{0,16},{4,20},{8,24},{12,28},{16,0},{20,4},{24,8},{28,12},{32,48},... | collective-permute-start | bytes 786440 | tf_op jit(solution)/shard_map/ppermute | solution.py:11
  502.5 46.8 %collective-permute-start.39 = (f32[256,256]{1,0:T(8,128)S(1)}, f32[256,256]{1,0:T(8,128)S(1)}, u32[]{:S(2)}, u32[]{:S(2)}) collective-permute-start(f32[256,256]{1,0:T(8,128)S(1)} %slice.2481), channel_id=1, source_target_pairs={{0,32},{4,36},{8,40},{12,44},{16,48},{20,52},{24,56},{28,60},{32,0... | collective-permute-start | bytes 786440 | tf_op jit(solution)/shard_map/ppermute | solution.py:11
  509.3 42.0 %collective-permute-start.44 = (f32[256,256]{1,0:T(8,128)S(1)}, f32[256,256]{1,0:T(8,128)S(1)}, u32[]{:S(2)}, u32[]{:S(2)}) collective-permute-start(f32[256,256]{1,0:T(8,128)S(1)} %slice.2493), channel_id=1, source_target_pairs={{0,64},{4,68},{8,72},{12,76},{16,80},{20,84},{24,88},{28,92},{32,9... | collective-permute-start | bytes 786440 | tf_op jit(solution)/shard_map/ppermute | solution.py:11
  512.8 46.5 %collective-permute-start.50 = (f32[256,256]{1,0:T(8,128)S(1)}, f32[256,256]{1,0:T(8,128)S(1)}, u32[]{:S(2)}, u32[]{:S(2)}) collective-permute-start(f32[256,256]{1,0:T(8,128)S(1)} %slice.2507), channel_id=1, source_target_pairs={{0,128},{4,132},{8,136},{12,140},{16,144},{20,148},{24,152},{28,15... | collective-permute-start | bytes 786440 | tf_op jit(solution)/shard_map/ppermute | solution.py:11
  525.9 35.6 %collective-permute-start.33 = (f32[128,256]{1,0:T(8,128)S(1)}, f32[128,256]{1,0:T(8,128)S(1)}, u32[]{:S(2)}, u32[]{:S(2)}) collective-permute-start(f32[128,256]{1,0:T(8,128)S(1)} %slice.2465), channel_id=1, source_target_pairs={{0,4},{4,0},{8,12},{12,8},{16,20},{20,16},{24,28},{28,24},{32,36},... | collective-permute-start | bytes 393224 | tf_op jit(solution)/shard_map/ppermute | solution.py:11
  547.4 15.1 %collective-permute-start.36 = (f32[128,256]{1,0:T(8,128)S(1)}, f32[128,256]{1,0:T(8,128)S(1)}, u32[]{:S(2)}, u32[]{:S(2)}) collective-permute-start(f32[128,256]{1,0:T(8,128)S(1)} %slice.2473), channel_id=1, source_target_pairs={{0,8},{4,12},{8,0},{12,4},{16,24},{20,28},{24,16},{28,20},{32,40},... | collective-permute-start | bytes 393224 | tf_op jit(solution)/shard_map/ppermute | solution.py:11
  549.4 26.1 %collective-permute-start.40 = (f32[128,256]{1,0:T(8,128)S(1)}, f32[128,256]{1,0:T(8,128)S(1)}, u32[]{:S(2)}, u32[]{:S(2)}) collective-permute-start(f32[128,256]{1,0:T(8,128)S(1)} %slice.2483), channel_id=1, source_target_pairs={{0,16},{4,20},{8,24},{12,28},{16,0},{20,4},{24,8},{28,12},{32,48},... | collective-permute-start | bytes 393224 | tf_op jit(solution)/shard_map/ppermute | solution.py:11
  551.4 26.1 %collective-permute-start.45 = (f32[128,256]{1,0:T(8,128)S(1)}, f32[128,256]{1,0:T(8,128)S(1)}, u32[]{:S(2)}, u32[]{:S(2)}) collective-permute-start(f32[128,256]{1,0:T(8,128)S(1)} %slice.2495), channel_id=1, source_target_pairs={{0,32},{4,36},{8,40},{12,44},{16,48},{20,52},{24,56},{28,60},{32,0... | collective-permute-start | bytes 393224 | tf_op jit(solution)/shard_map/ppermute | solution.py:11
  559.4 27.5 %collective-permute-start.51 = (f32[128,256]{1,0:T(8,128)S(1)}, f32[128,256]{1,0:T(8,128)S(1)}, u32[]{:S(2)}, u32[]{:S(2)}) collective-permute-start(f32[128,256]{1,0:T(8,128)S(1)} %slice.2509), channel_id=1, source_target_pairs={{0,64},{4,68},{8,72},{12,76},{16,80},{20,84},{24,88},{28,92},{32,9... | collective-permute-start | bytes 393224 | tf_op jit(solution)/shard_map/ppermute | solution.py:11
  562.5 32.5 %collective-permute-start.37 = (f32[64,256]{1,0:T(8,128)S(1)}, f32[64,256]{1,0:T(8,128)S(1)}, u32[]{:S(2)}, u32[]{:S(2)}) collective-permute-start(f32[64,256]{1,0:T(8,128)S(1)} %slice.2475), channel_id=1, source_target_pairs={{0,4},{4,0},{8,12},{12,8},{16,20},{20,16},{24,28},{28,24},{32,36},... | collective-permute-start | bytes 196616 | tf_op jit(solution)/shard_map/ppermute | solution.py:11
  575.5 20.3 %collective-permute-start.41 = (f32[64,256]{1,0:T(8,128)S(1)}, f32[64,256]{1,0:T(8,128)S(1)}, u32[]{:S(2)}, u32[]{:S(2)}) collective-permute-start(f32[64,256]{1,0:T(8,128)S(1)} %slice.2485), channel_id=1, source_target_pairs={{0,8},{4,12},{8,0},{12,4},{16,24},{20,28},{24,16},{28,20},{32,40},... | collective-permute-start | bytes 196616 | tf_op jit(solution)/shard_map/ppermute | solution.py:11
  577.5 20.3 %collective-permute-start.46 = (f32[64,256]{1,0:T(8,128)S(1)}, f32[64,256]{1,0:T(8,128)S(1)}, u32[]{:S(2)}, u32[]{:S(2)}) collective-permute-start(f32[64,256]{1,0:T(8,128)S(1)} %slice.2497), channel_id=1, source_target_pairs={{0,16},{4,20},{8,24},{12,28},{16,0},{20,4},{24,8},{28,12},{32,48},... | collective-permute-start | bytes 196616 | tf_op jit(solution)/shard_map/ppermute | solution.py:11
  587.0 16.9 %collective-permute-start.52 = (f32[64,256]{1,0:T(8,128)S(1)}, f32[64,256]{1,0:T(8,128)S(1)}, u32[]{:S(2)}, u32[]{:S(2)}) collective-permute-start(f32[64,256]{1,0:T(8,128)S(1)} %slice.2511), channel_id=1, source_target_pairs={{0,32},{4,36},{8,40},{12,44},{16,48},{20,52},{24,56},{28,60},{32,0... | collective-permute-start | bytes 196616 | tf_op jit(solution)/shard_map/ppermute | solution.py:11
  (125 other events, 241.0 us)
where the time goes:
time: 634 us; the launch traced here: 628 us
  starting transfers between devices  241 us (38%)
  local copies, waits for them, and re-layouts  133 us (21%)
  blocking collectives  98.5 us (16%)
  waiting for transfers between devices  54.5 us (9%)
  matrix products  47.1 us (7%)
  other arithmetic  29.4 us (5%)
  between operations  24.8 us (4%)
    ppermute x56, starting transfers between devices, partner(): lax.ppermute(array, axis, [(i, i ^ 1 << apart) for i in range(lax.axis_si...  241 us
    psum x1, blocking collectives, body(): scale_gradient = lax.psum(jnp.stack(scale_terms), ('seq', 'dp'))  98.5 us
    ppermute x56, waiting for transfers between devices, partner(): lax.ppermute(array, axis, [(i, i ^ 1 << apart) for i in range(lax.axis_si...  54.5 us
    unnamed x331, local copies, waits for them, and re-layouts  54 us
    concatenate x12, local copies, waits for them, and re-layouts, body(): jnp.concatenate([current, partner(current, 'seq', bit_num)], 0)  20.7 us
    dot_general x16, matrix products, body(): lax.dot_general(up_sel, val_sel, (((1,), (1,)), ((), ())), preferred_elem...  13.5 us
  transfers between devices with their start and end apart: 56, of which 11 were waited for; matrix products, arithmetic and copies ran while one was open for 29% of the time, Pallas kernels for 0%

commit v1 on v0

--- a/solution.py
+++ b/solution.py
@@ -1,3 +1,4 @@
+import functools
 import math
 import jax
 import jax.numpy as jnp
@@ -5,6 +6,14 @@
 from jax.sharding import PartitionSpec as P
 
 MIXER_CHANNELS = 16
+
+
+def link_samples_over_axis(arr, group_axis):
+    answer = lax.all_gather(arr, group_axis)
+    return jnp.sum(answer, axis=0)
+
+
+fix_boxes = functools.partial(link_samples_over_axis, group_axis=("seq", "dp"))
 
 
 def partner(array, axis, apart):
@@ -158,7 +167,7 @@
             val_part = own_grad[per_dev:, cols_lo : cols_lo + channel_extent]
             dk_cols.append(spread_rows(key_part.astype(jnp.bfloat16), dilation, offset))
             dv_cols.append(spread_rows(val_part.astype(jnp.bfloat16), dilation, offset))
-    scale_gradient = lax.psum(jnp.stack(scale_terms), ("seq", "dp"))
+    scale_gradient = fix_boxes(jnp.stack(scale_terms))
     attention_result = jnp.concatenate(out_cols, 1)[None]
     query_gradient = jnp.concatenate(dq_cols, 1)[None]
     key_gradient = jnp.concatenate(dk_cols, 1)[None]

time: 634 us -> 653 us (1.030)
  other arithmetic: 29.4 us -> 41.2 us
  local copies, waits for them, and re-layouts: 133 us -> 141 us
    unnamed x0 -> x1, blocking collectives: none -> 99.4 us
    psum x1 -> x0, blocking collectives: 98.5 us -> none  [body(): scale_gradient = lax.psum(jnp.stack(scale_terms), ('seq', 'dp'))]
    unnamed x331 -> x429, local copies, waits for them, and re-layouts: 54 us -> 58.2 us
  transfers between devices with their start and end apart: 56 -> 56, of which waited for: 11 -> 10; matrix products, arithmetic and copies ran while one was open for 29% -> 30% of each run, Pallas kernels for 0% -> 0%
where the time goes in v1:
time: 653 us; the launch traced here: 648 us
  starting transfers between devices  242 us (37%)
  local copies, waits for them, and re-layouts  141 us (22%)
  blocking collectives  99.4 us (15%)
  waiting for transfers between devices  50.8 us (8%)
  matrix products  48.8 us (7%)
  other arithmetic  41.2 us (6%)
  between operations  25.1 us (4%)
    ppermute x56, starting transfers between devices, partner(): lax.ppermute(array, axis, [(i, i ^ 1 << apart) for i in range(lax.axis_si...  242 us
    unnamed x1, blocking collectives  99.4 us
    unnamed x429, local copies, waits for them, and re-layouts  58.2 us
    ppermute x56, waiting for transfers between devices, partner(): lax.ppermute(array, axis, [(i, i ^ 1 << apart) for i in range(lax.axis_si...  50.8 us
    concatenate x12, local copies, waits for them, and re-layouts, body(): jnp.concatenate([current, partner(current, 'seq', bit_num)], 0)  18.7 us
    slice x36, local copies, waits for them, and re-layouts, select_rows(): column_block.reshape(tokens // dilation, dilation, channel_extent)  14.1 us
    dot_general x16, matrix products, body(): lax.dot_general(up_sel, val_sel, (((1,), (1,)), ((), ())), preferred_elem...  13.9 us
  transfers between devices with their start and end apart: 56, of which 10 were waited for; matrix products, arithmetic and copies ran while one was open for 30% of the time, Pallas kernels for 0%

profile of v1, /device:TPU:4, one launch (start us, length us, event | category | flops | bytes accessed | tf_op | source)
XLA Modules:
  0.0 647.7 jit_solution(17001866790490246314)
XLA Ops:
  2.6 3.8 collective-permute-start.21
  10.5 3.8 collective-permute-start.10
  17.8 3.8 collective-permute-start.3
  82.1 5.2 collective-permute-start.22
  89.3 3.8 collective-permute-start
  93.2 4.4 collective-permute-start.16
  99.7 9.1 %collective-permute-start.23 = (bf16[32,256]{1,0:T(8,128)(2,1)S(1)}, bf16[32,256]{1,0:T(8,128)(2,1)S(1)}, u32[]{:S(2)}, u32[]{:S(2)}) collective-permute-start(bf16[32,256]{1,0:T(8,128)(2,1)S(1)} %pad_maximum_fusion.36), channel_id=1, source_target_pairs={{0,16},{4,20},{8,24},{12,28},{16,0},{20,4},{24,8},{28,12},{32,48},... | collective-permute-start | bytes 49160 | tf_op jit(solution)/shard_map/ppermute | solution.py:20
  110.5 4.4 collective-permute-start.11
  114.9 7.9 %collective-permute-start.17 = (bf16[64,256]{1,0:T(8,128)(2,1)S(1)}, bf16[64,256]{1,0:T(8,128)(2,1)S(1)}, u32[]{:S(2)}, u32[]{:S(2)}) collective-permute-start(bf16[64,256]{1,0:T(8,128)(2,1)S(1)} %pad_maximum_fusion.32), channel_id=1, source_target_pairs={{0,16},{4,20},{8,24},{12,28},{16,0},{20,4},{24,8},{28,12},{32,48},... | collective-permute-start | bytes 98312 | tf_op jit(solution)/shard_map/ppermute | solution.py:20
  123.5 8.1 %collective-permute-start.24 = (bf16[64,256]{1,0:T(8,128)(2,1)S(1)}, bf16[64,256]{1,0:T(8,128)(2,1)S(1)}, u32[]{:S(2)}, u32[]{:S(2)}) collective-permute-start(bf16[64,256]{1,0:T(8,128)(2,1)S(1)} %concatenate.419), channel_id=1, source_target_pairs={{0,32},{4,36},{8,40},{12,44},{16,48},{20,52},{24,56},{28,60},{32,0... | collective-permute-start | bytes 98312 | tf_op jit(solution)/shard_map/ppermute | solution.py:20
  132.3 3.4 collective-permute-start.7
  138.1 3.7 collective-permute-start.12
  141.8 10.2 %collective-permute-start.18 = (bf16[128,256]{1,0:T(8,128)(2,1)}, bf16[128,256]{1,0:T(8,128)(2,1)S(1)}, u32[]{:S(2)}, u32[]{:S(2)}) collective-permute-start(bf16[128,256]{1,0:T(8,128)(2,1)} %get-tuple-element.952), channel_id=1, source_target_pairs={{0,32},{4,36},{8,40},{12,44},{16,48},{20,52},{24,56},{28,60},{32,0... | collective-permute-start | bytes 196616 | tf_op jit(solution)/shard_map/ppermute | solution.py:20
  152.7 3.5 collective-permute-start.25
  157.5 3.0 collective-permute-start.4
  161.2 4.2 collective-permute-start.8
  166.2 6.2 collective-permute-start.13
  172.3 3.6 concatenate.421
  176.0 3.6 collective-permute-start.19
  184.4 4.9 collective-permute-start.26
  190.2 2.9 collective-permute-start.2
  193.9 6.4 collective-permute-start.5
  201.8 7.3 %collective-permute-start.9 = (bf16[512,256]{1,0:T(8,128)(2,1)}, bf16[512,256]{1,0:T(8,128)(2,1)}, u32[]{:S(2)}, u32[]{:S(2)}) collective-permute-start(bf16[512,256]{1,0:T(8,128)(2,1)} %get-tuple-element.925), channel_id=1, source_target_pairs={{0,32},{4,36},{8,40},{12,44},{16,48},{20,52},{24,56},{28,60},{32,0... | collective-permute-start | bytes 786440 | tf_op jit(solution)/shard_map/ppermute | solution.py:20
  215.0 3.7 collective-permute-start.20
  218.7 4.3 concatenate.422
  297.4 6.6 %collective-permute-start.31 = (f32[512,256]{1,0:T(8,128)}, f32[512,256]{1,0:T(8,128)}, u32[]{:S(2)}, u32[]{:S(2)}) collective-permute-start(f32[512,256]{1,0:T(8,128)} %bitcast.190), channel_id=1, source_target_pairs={{0,16},{4,20},{8,24},{12,28},{16,0},{20,4},{24,8},{28,12},{32,48},... | collective-permute-start | bytes 1572872 | tf_op jit(solution)/shard_map/ppermute | solution.py:20
  324.6 5.6 collective-permute-start.34
  352.8 4.3 collective-permute-start.38
  386.3 99.4 %all-reduce.40 = f32[8192]{0:T(1024)S(1)} all-reduce(f32[8192]{0:T(1024)S(1)} %dynamic-update-slice.168), channel_id=2, replica_groups=mesh['seq'=128,'dp'=4] {'seq','dp'}, use_global_device_ids=true, to_apply=%add.40 | all-reduce | flops 8192 | bytes 65536
  495.7 3.1 collective-permute-start.43
  500.5 4.3 collective-permute-start.49
  505.9 4.0 collective-permute-start.30
  514.9 4.8 collective-permute-start.35
  520.9 7.3 %collective-permute-start.39 = (f32[256,256]{1,0:T(8,128)S(1)}, f32[256,256]{1,0:T(8,128)S(1)}, u32[]{:S(2)}, u32[]{:S(2)}) collective-permute-start(f32[256,256]{1,0:T(8,128)S(1)} %slice.2481), channel_id=1, source_target_pairs={{0,32},{4,36},{8,40},{12,44},{16,48},{20,52},{24,56},{28,60},{32,0... | collective-permute-start | bytes 786440 | tf_op jit(solution)/shard_map/ppermute | solution.py:20
  528.3 3.4 collective-permute-start.44
  531.9 3.9 collective-permute-start.50
  536.5 6.9 %collective-permute-done.32 = f32[256,256]{1,0:T(8,128)S(1)} collective-permute-done((f32[256,256]{1,0:T(8,128)S(1)}, f32[256,256]{1,0:T(8,128)S(1)}, u32[]{:S(2)}, u32[]{:S(2)}) %collective-permute-start.32) | collective-permute-done | bytes 262176 | tf_op jit(solution)/shard_map/ppermute | solution.py:20
  545.4 20.2 %collective-permute-done.35 = f32[256,256]{1,0:T(8,128)S(1)} collective-permute-done((f32[256,256]{1,0:T(8,128)S(1)}, f32[256,256]{1,0:T(8,128)S(1)}, u32[]{:S(2)}, u32[]{:S(2)}) %collective-permute-start.35) | collective-permute-done | bytes 262176 | tf_op jit(solution)/shard_map/ppermute | solution.py:20
  569.7 7.9 %collective-permute-start.45 = (f32[128,256]{1,0:T(8,128)S(1)}, f32[128,256]{1,0:T(8,128)S(1)}, u32[]{:S(2)}, u32[]{:S(2)}) collective-permute-start(f32[128,256]{1,0:T(8,128)S(1)} %slice.2495), channel_id=1, source_target_pairs={{0,32},{4,36},{8,40},{12,44},{16,48},{20,52},{24,56},{28,60},{32,0... | collective-permute-start | bytes 393224 | tf_op jit(solution)/shard_map/ppermute | solution.py:20
  577.7 3.2 collective-permute-start.51
  581.9 9.4 %collective-permute-start.37 = (f32[64,256]{1,0:T(8,128)S(1)}, f32[64,256]{1,0:T(8,128)S(1)}, u32[]{:S(2)}, u32[]{:S(2)}) collective-permute-start(f32[64,256]{1,0:T(8,128)S(1)} %slice.2475), channel_id=1, source_target_pairs={{0,4},{4,0},{8,12},{12,8},{16,20},{20,16},{24,28},{28,24},{32,36},... | collective-permute-start | bytes 196616 | tf_op jit(solution)/shard_map/ppermute | solution.py:20
  591.3 3.3 collective-permute-done.40
  596.6 10.3 %collective-permute-start.46 = (f32[64,256]{1,0:T(8,128)S(1)}, f32[64,256]{1,0:T(8,128)S(1)}, u32[]{:S(2)}, u32[]{:S(2)}) collective-permute-start(f32[64,256]{1,0:T(8,128)S(1)} %slice.2497), channel_id=1, source_target_pairs={{0,16},{4,20},{8,24},{12,28},{16,0},{20,4},{24,8},{28,12},{32,48},... | collective-permute-start | bytes 196616 | tf_op jit(solution)/shard_map/ppermute | solution.py:20
  607.0 6.5 %collective-permute-start.52 = (f32[64,256]{1,0:T(8,128)S(1)}, f32[64,256]{1,0:T(8,128)S(1)}, u32[]{:S(2)}, u32[]{:S(2)}) collective-permute-start(f32[64,256]{1,0:T(8,128)S(1)} %slice.2511), channel_id=1, source_target_pairs={{0,32},{4,36},{8,40},{12,44},{16,48},{20,52},{24,56},{28,60},{32,0... | collective-permute-start | bytes 196616 | tf_op jit(solution)/shard_map/ppermute | solution.py:20
  618.2 4.9 collective-permute-done.52
  628.4 4.5 collective-permute-done.53
  636.0 3.5 collective-permute-done.54
  641.4 3.6 collective-permute-done.55
  (963 shorter events, 266.4 us)
Async XLA Ops:
  2.6 77.4 %collective-permute-start.21 = (bf16[8,256]{1,0:T(8,128)(2,1)}, bf16[8,256]{1,0:T(8,128)(2,1)S(1)}, u32[]{:S(2)}, u32[]{:S(2)}) collective-permute-start(bf16[8,256]{1,0:T(8,128)(2,1)} %maximum_maximum_fusion.4), channel_id=1, source_target_pairs={{0,4},{4,0},{8,12},{12,8},{16,20},{20,16},{24,28},{28,24},{32,36},... | collective-permute-start | bytes 12296 | tf_op jit(solution)/shard_map/ppermute | solution.py:20
  7.7 74.3 %collective-permute-start.15 = (bf16[16,256]{1,0:T(8,128)(2,1)}, bf16[16,256]{1,0:T(8,128)(2,1)}, u32[]{:S(2)}, u32[]{:S(2)}) collective-permute-start(bf16[16,256]{1,0:T(8,128)(2,1)} %maximum_maximum_fusion.3), channel_id=1, source_target_pairs={{0,4},{4,0},{8,12},{12,8},{16,20},{20,16},{24,28},{28,24},{32,36},... | collective-permute-start | bytes 24584 | tf_op jit(solution)/shard_map/ppermute | solution.py:20
  10.5 82.7 %collective-permute-start.10 = (bf16[32,256]{1,0:T(8,128)(2,1)}, bf16[32,256]{1,0:T(8,128)(2,1)S(1)}, u32[]{:S(2)}, u32[]{:S(2)}) collective-permute-start(bf16[32,256]{1,0:T(8,128)(2,1)} %maximum_maximum_fusion.2), channel_id=1, source_target_pairs={{0,4},{4,0},{8,12},{12,8},{16,20},{20,16},{24,28},{28,24},{32,36},... | collective-permute-start | bytes 49160 | tf_op jit(solution)/shard_map/ppermute | solution.py:20
  15.0 99.9 %collective-permute-start.6 = (bf16[64,256]{1,0:T(8,128)(2,1)}, bf16[64,256]{1,0:T(8,128)(2,1)S(1)}, u32[]{:S(2)}, u32[]{:S(2)}) collective-permute-start(bf16[64,256]{1,0:T(8,128)(2,1)} %maximum_maximum_fusion.1), channel_id=1, source_target_pairs={{0,4},{4,0},{8,12},{12,8},{16,20},{20,16},{24,28},{28,24},{32,36},... | collective-permute-start | bytes 98312 | tf_op jit(solution)/shard_map/ppermute | solution.py:20
  17.8 124.0 %collective-permute-start.3 = (bf16[128,256]{1,0:T(8,128)(2,1)}, bf16[128,256]{1,0:T(8,128)(2,1)S(1)}, u32[]{:S(2)}, u32[]{:S(2)}) collective-permute-start(bf16[128,256]{1,0:T(8,128)(2,1)} %maximum_maximum_fusion), channel_id=1, source_target_pairs={{0,4},{4,0},{8,12},{12,8},{16,20},{20,16},{24,28},{28,24},{32,36},... | collective-permute-start | bytes 196616 | tf_op jit(solution)/shard_map/ppermute | solution.py:20
  80.0 103.8 %collective-permute-start.1 = (bf16[256,256]{1,0:T(8,128)(2,1)}, bf16[256,256]{1,0:T(8,128)(2,1)}, u32[]{:S(2)}, u32[]{:S(2)}) collective-permute-start(bf16[256,256]{1,0:T(8,128)(2,1)} %pad_maximum_fusion.26), channel_id=1, source_target_pairs={{0,4},{4,0},{8,12},{12,8},{16,20},{20,16},{24,28},{28,24},{32,36},... | collective-permute-start | bytes 393224 | tf_op jit(solution)/shard_map/ppermute | solution.py:20
  89.3 86.7 %collective-permute-start = (bf16[256,256]{1,0:T(8,128)(2,1)S(1)}, bf16[256,256]{1,0:T(8,128)(2,1)S(1)}, u32[]{:S(2)}, u32[]{:S(2)}) collective-permute-start(bf16[256,256]{1,0:T(8,128)(2,1)S(1)} %pad_maximum_fusion.25), channel_id=1, source_target_pairs={{0,4},{4,0},{8,12},{12,8},{16,20},{20,16},{24,28},{28,24},{32,36},... | collective-permute-start | bytes 393224 | tf_op jit(solution)/shard_map/ppermute | solution.py:20
  110.5 13.0 %collective-permute-start.11 = (bf16[64,256]{1,0:T(8,128)(2,1)S(1)}, bf16[64,256]{1,0:T(8,128)(2,1)S(1)}, u32[]{:S(2)}, u32[]{:S(2)}) collective-permute-start(bf16[64,256]{1,0:T(8,128)(2,1)S(1)} %pad_maximum_fusion.31), channel_id=1, source_target_pairs={{0,8},{4,12},{8,0},{12,4},{16,24},{20,28},{24,16},{28,20},{32,40},... | collective-permute-start | bytes 98312 | tf_op jit(solution)/shard_map/ppermute | solution.py:20
  114.9 17.4 %collective-permute-start.17 = (bf16[64,256]{1,0:T(8,128)(2,1)S(1)}, bf16[64,256]{1,0:T(8,128)(2,1)S(1)}, u32[]{:S(2)}, u32[]{:S(2)}) collective-permute-start(bf16[64,256]{1,0:T(8,128)(2,1)S(1)} %pad_maximum_fusion.32), channel_id=1, source_target_pairs={{0,16},{4,20},{8,24},{12,28},{16,0},{20,4},{24,8},{28,12},{32,48},... | collective-permute-start | bytes 98312 | tf_op jit(solution)/shard_map/ppermute | solution.py:20
  123.5 14.6 %collective-permute-start.24 = (bf16[64,256]{1,0:T(8,128)(2,1)S(1)}, bf16[64,256]{1,0:T(8,128)(2,1)S(1)}, u32[]{:S(2)}, u32[]{:S(2)}) collective-permute-start(bf16[64,256]{1,0:T(8,128)(2,1)S(1)} %concatenate.419), channel_id=1, source_target_pairs={{0,32},{4,36},{8,40},{12,44},{16,48},{20,52},{24,56},{28,60},{32,0... | collective-permute-start | bytes 98312 | tf_op jit(solution)/shard_map/ppermute | solution.py:20
  132.3 20.4 %collective-permute-start.7 = (bf16[128,256]{1,0:T(8,128)(2,1)S(1)}, bf16[128,256]{1,0:T(8,128)(2,1)S(1)}, u32[]{:S(2)}, u32[]{:S(2)}) collective-permute-start(bf16[128,256]{1,0:T(8,128)(2,1)S(1)} %pad_maximum_fusion.29), channel_id=1, source_target_pairs={{0,8},{4,12},{8,0},{12,4},{16,24},{20,28},{24,16},{28,20},{32,40},... | collective-permute-start | bytes 196616 | tf_op jit(solution)/shard_map/ppermute | solution.py:20
  138.1 19.4 %collective-permute-start.12 = (bf16[128,256]{1,0:T(8,128)(2,1)S(1)}, bf16[128,256]{1,0:T(8,128)(2,1)S(1)}, u32[]{:S(2)}, u32[]{:S(2)}) collective-permute-start(bf16[128,256]{1,0:T(8,128)(2,1)S(1)} %pad_maximum_fusion.30), channel_id=1, source_target_pairs={{0,16},{4,20},{8,24},{12,28},{16,0},{20,4},{24,8},{28,12},{32,48},... | collective-permute-start | bytes 196616 | tf_op jit(solution)/shard_map/ppermute | solution.py:20
  141.8 19.4 %collective-permute-start.18 = (bf16[128,256]{1,0:T(8,128)(2,1)}, bf16[128,256]{1,0:T(8,128)(2,1)S(1)}, u32[]{:S(2)}, u32[]{:S(2)}) collective-permute-start(bf16[128,256]{1,0:T(8,128)(2,1)} %get-tuple-element.952), channel_id=1, source_target_pairs={{0,32},{4,36},{8,40},{12,44},{16,48},{20,52},{24,56},{28,60},{32,0... | collective-permute-start | bytes 196616 | tf_op jit(solution)/shard_map/ppermute | solution.py:20
  152.7 13.5 %collective-permute-start.25 = (bf16[128,256]{1,0:T(8,128)(2,1)S(1)}, bf16[128,256]{1,0:T(8,128)(2,1)S(1)}, u32[]{:S(2)}, u32[]{:S(2)}) collective-permute-start(bf16[128,256]{1,0:T(8,128)(2,1)S(1)} %concatenate.420), channel_id=1, source_target_pairs={{0,64},{4,68},{8,72},{12,76},{16,80},{20,84},{24,88},{28,92},{32,9... | collective-permute-start | bytes 196616 | tf_op jit(solution)/shard_map/ppermute | solution.py:20
  157.5 32.7 %collective-permute-start.4 = (bf16[256,256]{1,0:T(8,128)(2,1)}, bf16[256,256]{1,0:T(8,128)(2,1)S(1)}, u32[]{:S(2)}, u32[]{:S(2)}) collective-permute-start(bf16[256,256]{1,0:T(8,128)(2,1)} %pad_maximum_fusion.27), channel_id=1, source_target_pairs={{0,8},{4,12},{8,0},{12,4},{16,24},{20,28},{24,16},{28,20},{32,40},... | collective-permute-start | bytes 393224 | tf_op jit(solution)/shard_map/ppermute | solution.py:20
  161.2 32.7 %collective-permute-start.8 = (bf16[256,256]{1,0:T(8,128)(2,1)}, bf16[256,256]{1,0:T(8,128)(2,1)}, u32[]{:S(2)}, u32[]{:S(2)}) collective-permute-start(bf16[256,256]{1,0:T(8,128)(2,1)} %pad_maximum_fusion.28), channel_id=1, source_target_pairs={{0,16},{4,20},{8,24},{12,28},{16,0},{20,4},{24,8},{28,12},{32,48},... | collective-permute-start | bytes 393224 | tf_op jit(solution)/shard_map/ppermute | solution.py:20
  166.2 35.6 %collective-permute-start.13 = (bf16[256,256]{1,0:T(8,128)(2,1)}, bf16[256,256]{1,0:T(8,128)(2,1)}, u32[]{:S(2)}, u32[]{:S(2)}) collective-permute-start(bf16[256,256]{1,0:T(8,128)(2,1)} %get-tuple-element.938), channel_id=1, source_target_pairs={{0,32},{4,36},{8,40},{12,44},{16,48},{20,52},{24,56},{28,60},{32,0... | collective-permute-start | bytes 393224 | tf_op jit(solution)/shard_map/ppermute | solution.py:20
  176.0 34.7 %collective-permute-start.19 = (bf16[256,256]{1,0:T(8,128)(2,1)}, bf16[256,256]{1,0:T(8,128)(2,1)}, u32[]{:S(2)}, u32[]{:S(2)}) collective-permute-start(bf16[256,256]{1,0:T(8,128)(2,1)} %get-tuple-element.935), channel_id=1, source_target_pairs={{0,64},{4,68},{8,72},{12,76},{16,80},{20,84},{24,88},{28,92},{32,9... | collective-permute-start | bytes 393224 | tf_op jit(solution)/shard_map/ppermute | solution.py:20
  184.4 30.6 %collective-permute-start.26 = (bf16[256,256]{1,0:T(8,128)(2,1)S(1)}, bf16[256,256]{1,0:T(8,128)(2,1)S(1)}, u32[]{:S(2)}, u32[]{:S(2)}) collective-permute-start(bf16[256,256]{1,0:T(8,128)(2,1)S(1)} %copy-done.28), channel_id=1, source_target_pairs={{0,128},{4,132},{8,136},{12,140},{16,144},{20,148},{24,152},{28,15... | collective-permute-start | bytes 393224 | tf_op jit(solution)/shard_map/ppermute | solution.py:20
  190.2 32.8 %collective-permute-start.2 = (bf16[512,256]{1,0:T(8,128)(2,1)S(1)}, bf16[512,256]{1,0:T(8,128)(2,1)}, u32[]{:S(2)}, u32[]{:S(2)}) collective-permute-start(bf16[512,256]{1,0:T(8,128)(2,1)S(1)} %pad_maximum_fusion.20), channel_id=1, source_target_pairs={{0,8},{4,12},{8,0},{12,4},{16,24},{20,28},{24,16},{28,20},{32,40},... | collective-permute-start | bytes 786440 | tf_op jit(solution)/shard_map/ppermute | solution.py:20
  193.9 64.8 %collective-permute-start.5 = (bf16[512,256]{1,0:T(8,128)(2,1)}, bf16[512,256]{1,0:T(8,128)(2,1)}, u32[]{:S(2)}, u32[]{:S(2)}) collective-permute-start(bf16[512,256]{1,0:T(8,128)(2,1)} %pad_maximum_fusion.21), channel_id=1, source_target_pairs={{0,16},{4,20},{8,24},{12,28},{16,0},{20,4},{24,8},{28,12},{32,48},... | collective-permute-start | bytes 786440 | tf_op jit(solution)/shard_map/ppermute | solution.py:20
  201.8 73.8 %collective-permute-start.9 = (bf16[512,256]{1,0:T(8,128)(2,1)}, bf16[512,256]{1,0:T(8,128)(2,1)}, u32[]{:S(2)}, u32[]{:S(2)}) collective-permute-start(bf16[512,256]{1,0:T(8,128)(2,1)} %get-tuple-element.925), channel_id=1, source_target_pairs={{0,32},{4,36},{8,40},{12,44},{16,48},{20,52},{24,56},{28,60},{32,0... | collective-permute-start | bytes 786440 | tf_op jit(solution)/shard_map/ppermute | solution.py:20
  210.7 86.6 %collective-permute-start.14 = (bf16[512,256]{1,0:T(8,128)(2,1)}, bf16[512,256]{1,0:T(8,128)(2,1)}, u32[]{:S(2)}, u32[]{:S(2)}) collective-permute-start(bf16[512,256]{1,0:T(8,128)(2,1)} %get-tuple-element.923), channel_id=1, source_target_pairs={{0,64},{4,68},{8,72},{12,76},{16,80},{20,84},{24,88},{28,92},{32,9... | collective-permute-start | bytes 786440 | tf_op jit(solution)/shard_map/ppermute | solution.py:20
  215.0 109.6 %collective-permute-start.20 = (bf16[512,256]{1,0:T(8,128)(2,1)}, bf16[512,256]{1,0:T(8,128)(2,1)}, u32[]{:S(2)}, u32[]{:S(2)}) collective-permute-start(bf16[512,256]{1,0:T(8,128)(2,1)} %get-tuple-element.921), channel_id=1, source_target_pairs={{0,128},{4,132},{8,136},{12,140},{16,144},{20,148},{24,152},{28,15... | collective-permute-start | bytes 786440 | tf_op jit(solution)/shard_map/ppermute | solution.py:20
  223.1 129.8 %collective-permute-start.27 = (bf16[512,256]{1,0:T(8,128)(2,1)}, bf16[512,256]{1,0:T(8,128)(2,1)}, u32[]{:S(2)}, u32[]{:S(2)}) collective-permute-start(bf16[512,256]{1,0:T(8,128)(2,1)} %concatenate.422), channel_id=1, source_target_pairs={{0,256},{4,260},{8,264},{12,268},{16,272},{20,276},{24,280},{28,28... | collective-permute-start | bytes 786440 | tf_op jit(solution)/shard_map/ppermute | solution.py:20
  258.6 241.8 %collective-permute-start.29 = (f32[512,256]{0,1:T(8,128)}, f32[512,256]{0,1:T(8,128)}, u32[]{:S(2)}, u32[]{:S(2)}) collective-permute-start(f32[512,256]{0,1:T(8,128)} %slice.2212), channel_id=1, source_target_pairs={{0,8},{4,12},{8,0},{12,4},{16,24},{20,28},{24,16},{28,20},{32,40},... | collective-permute-start | bytes 1572872 | tf_op jit(solution)/shard_map/ppermute | solution.py:20
  275.6 220.1 %collective-permute-start.28 = (f32[256,256]{0,1:T(8,128)}, f32[256,256]{0,1:T(8,128)}, u32[]{:S(2)}, u32[]{:S(2)}) collective-permute-start(f32[256,256]{0,1:T(8,128)} %bitcast.622), channel_id=1, source_target_pairs={{0,4},{4,0},{8,12},{12,8},{16,20},{20,16},{24,28},{28,24},{32,36},... | collective-permute-start | bytes 786440 | tf_op jit(solution)/shard_map/ppermute | solution.py:20
  297.4 208.5 %collective-permute-start.31 = (f32[512,256]{1,0:T(8,128)}, f32[512,256]{1,0:T(8,128)}, u32[]{:S(2)}, u32[]{:S(2)}) collective-permute-start(f32[512,256]{1,0:T(8,128)} %bitcast.190), channel_id=1, source_target_pairs={{0,16},{4,20},{8,24},{12,28},{16,0},{20,4},{24,8},{28,12},{32,48},... | collective-permute-start | bytes 1572872 | tf_op jit(solution)/shard_map/ppermute | solution.py:20
  324.6 186.4 %collective-permute-start.34 = (f32[512,256]{1,0:T(8,128)}, f32[512,256]{1,0:T(8,128)}, u32[]{:S(2)}, u32[]{:S(2)}) collective-permute-start(f32[512,256]{1,0:T(8,128)} %bitcast.694), channel_id=1, source_target_pairs={{0,32},{4,36},{8,40},{12,44},{16,48},{20,52},{24,56},{28,60},{32,0... | collective-permute-start | bytes 1572872 | tf_op jit(solution)/shard_map/ppermute | solution.py:20
  352.8 162.1 %collective-permute-start.38 = (f32[512,256]{1,0:T(8,128)}, f32[512,256]{1,0:T(8,128)}, u32[]{:S(2)}, u32[]{:S(2)}) collective-permute-start(f32[512,256]{1,0:T(8,128)} %bitcast.206), channel_id=1, source_target_pairs={{0,64},{4,68},{8,72},{12,76},{16,80},{20,84},{24,88},{28,92},{32,9... | collective-permute-start | bytes 1572872 | tf_op jit(solution)/shard_map/ppermute | solution.py:20
  495.7 25.2 %collective-permute-start.43 = (f32[512,256]{1,0:T(8,128)}, f32[512,256]{1,0:T(8,128)S(1)}, u32[]{:S(2)}, u32[]{:S(2)}) collective-permute-start(f32[512,256]{1,0:T(8,128)} %bitcast.695), channel_id=1, source_target_pairs={{0,128},{4,132},{8,136},{12,140},{16,144},{20,148},{24,152},{28,15... | collective-permute-start | bytes 1572872 | tf_op jit(solution)/shard_map/ppermute | solution.py:20
  500.5 27.8 %collective-permute-start.49 = (f32[512,256]{1,0:T(8,128)S(1)}, f32[512,256]{1,0:T(8,128)S(1)}, u32[]{:S(2)}, u32[]{:S(2)}) collective-permute-start(f32[512,256]{1,0:T(8,128)S(1)} %copy-done.13), channel_id=1, source_target_pairs={{0,256},{4,260},{8,264},{12,268},{16,272},{20,276},{24,280},{28,28... | collective-permute-start | bytes 1572872 | tf_op jit(solution)/shard_map/ppermute | solution.py:20
  505.9 26.0 %collective-permute-start.30 = (f32[256,256]{0,1:T(8,128)S(1)}, f32[256,256]{0,1:T(8,128)S(1)}, u32[]{:S(2)}, u32[]{:S(2)}) collective-permute-start(f32[256,256]{0,1:T(8,128)S(1)} %slice.2458), channel_id=1, source_target_pairs={{0,4},{4,0},{8,12},{12,8},{16,20},{20,16},{24,28},{28,24},{32,36},... | collective-permute-start | bytes 786440 | tf_op jit(solution)/shard_map/ppermute | solution.py:20
  511.0 32.5 %collective-permute-start.32 = (f32[256,256]{1,0:T(8,128)S(1)}, f32[256,256]{1,0:T(8,128)S(1)}, u32[]{:S(2)}, u32[]{:S(2)}) collective-permute-start(f32[256,256]{1,0:T(8,128)S(1)} %slice.2463), channel_id=1, source_target_pairs={{0,8},{4,12},{8,0},{12,4},{16,24},{20,28},{24,16},{28,20},{32,40},... | collective-permute-start | bytes 786440 | tf_op jit(solution)/shard_map/ppermute | solution.py:20
  514.9 50.7 %collective-permute-start.35 = (f32[256,256]{1,0:T(8,128)S(1)}, f32[256,256]{1,0:T(8,128)S(1)}, u32[]{:S(2)}, u32[]{:S(2)}) collective-permute-start(f32[256,256]{1,0:T(8,128)S(1)} %slice.2471), channel_id=1, source_target_pairs={{0,16},{4,20},{8,24},{12,28},{16,0},{20,4},{24,8},{28,12},{32,48},... | collective-permute-start | bytes 786440 | tf_op jit(solution)/shard_map/ppermute | solution.py:20
  520.9 46.8 %collective-permute-start.39 = (f32[256,256]{1,0:T(8,128)S(1)}, f32[256,256]{1,0:T(8,128)S(1)}, u32[]{:S(2)}, u32[]{:S(2)}) collective-permute-start(f32[256,256]{1,0:T(8,128)S(1)} %slice.2481), channel_id=1, source_target_pairs={{0,32},{4,36},{8,40},{12,44},{16,48},{20,52},{24,56},{28,60},{32,0... | collective-permute-start | bytes 786440 | tf_op jit(solution)/shard_map/ppermute | solution.py:20
  528.3 41.3 %collective-permute-start.44 = (f32[256,256]{1,0:T(8,128)S(1)}, f32[256,256]{1,0:T(8,128)S(1)}, u32[]{:S(2)}, u32[]{:S(2)}) collective-permute-start(f32[256,256]{1,0:T(8,128)S(1)} %slice.2493), channel_id=1, source_target_pairs={{0,64},{4,68},{8,72},{12,76},{16,80},{20,84},{24,88},{28,92},{32,9... | collective-permute-start | bytes 786440 | tf_op jit(solution)/shard_map/ppermute | solution.py:20
  531.9 45.8 %collective-permute-start.50 = (f32[256,256]{1,0:T(8,128)S(1)}, f32[256,256]{1,0:T(8,128)S(1)}, u32[]{:S(2)}, u32[]{:S(2)}) collective-permute-start(f32[256,256]{1,0:T(8,128)S(1)} %slice.2507), channel_id=1, source_target_pairs={{0,128},{4,132},{8,136},{12,140},{16,144},{20,148},{24,152},{28,15... | collective-permute-start | bytes 786440 | tf_op jit(solution)/shard_map/ppermute | solution.py:20
  543.5 37.4 %collective-permute-start.33 = (f32[128,256]{1,0:T(8,128)S(1)}, f32[128,256]{1,0:T(8,128)S(1)}, u32[]{:S(2)}, u32[]{:S(2)}) collective-permute-start(f32[128,256]{1,0:T(8,128)S(1)} %slice.2465), channel_id=1, source_target_pairs={{0,4},{4,0},{8,12},{12,8},{16,20},{20,16},{24,28},{28,24},{32,36},... | collective-permute-start | bytes 393224 | tf_op jit(solution)/shard_map/ppermute | solution.py:20
  565.7 16.2 %collective-permute-start.36 = (f32[128,256]{1,0:T(8,128)S(1)}, f32[128,256]{1,0:T(8,128)S(1)}, u32[]{:S(2)}, u32[]{:S(2)}) collective-permute-start(f32[128,256]{1,0:T(8,128)S(1)} %slice.2473), channel_id=1, source_target_pairs={{0,8},{4,12},{8,0},{12,4},{16,24},{20,28},{24,16},{28,20},{32,40},... | collective-permute-start | bytes 393224 | tf_op jit(solution)/shard_map/ppermute | solution.py:20
  567.7 26.9 %collective-permute-start.40 = (f32[128,256]{1,0:T(8,128)S(1)}, f32[128,256]{1,0:T(8,128)S(1)}, u32[]{:S(2)}, u32[]{:S(2)}) collective-permute-start(f32[128,256]{1,0:T(8,128)S(1)} %slice.2483), channel_id=1, source_target_pairs={{0,16},{4,20},{8,24},{12,28},{16,0},{20,4},{24,8},{28,12},{32,48},... | collective-permute-start | bytes 393224 | tf_op jit(solution)/shard_map/ppermute | solution.py:20
  569.7 26.8 %collective-permute-start.45 = (f32[128,256]{1,0:T(8,128)S(1)}, f32[128,256]{1,0:T(8,128)S(1)}, u32[]{:S(2)}, u32[]{:S(2)}) collective-permute-start(f32[128,256]{1,0:T(8,128)S(1)} %slice.2495), channel_id=1, source_target_pairs={{0,32},{4,36},{8,40},{12,44},{16,48},{20,52},{24,56},{28,60},{32,0... | collective-permute-start | bytes 393224 | tf_op jit(solution)/shard_map/ppermute | solution.py:20
  577.7 29.2 %collective-permute-start.51 = (f32[128,256]{1,0:T(8,128)S(1)}, f32[128,256]{1,0:T(8,128)S(1)}, u32[]{:S(2)}, u32[]{:S(2)}) collective-permute-start(f32[128,256]{1,0:T(8,128)S(1)} %slice.2509), channel_id=1, source_target_pairs={{0,64},{4,68},{8,72},{12,76},{16,80},{20,84},{24,88},{28,92},{32,9... | collective-permute-start | bytes 393224 | tf_op jit(solution)/shard_map/ppermute | solution.py:20
  581.9 31.6 %collective-permute-start.37 = (f32[64,256]{1,0:T(8,128)S(1)}, f32[64,256]{1,0:T(8,128)S(1)}, u32[]{:S(2)}, u32[]{:S(2)}) collective-permute-start(f32[64,256]{1,0:T(8,128)S(1)} %slice.2475), channel_id=1, source_target_pairs={{0,4},{4,0},{8,12},{12,8},{16,20},{20,16},{24,28},{28,24},{32,36},... | collective-permute-start | bytes 196616 | tf_op jit(solution)/shard_map/ppermute | solution.py:20
  594.6 19.7 %collective-permute-start.41 = (f32[64,256]{1,0:T(8,128)S(1)}, f32[64,256]{1,0:T(8,128)S(1)}, u32[]{:S(2)}, u32[]{:S(2)}) collective-permute-start(f32[64,256]{1,0:T(8,128)S(1)} %slice.2485), channel_id=1, source_target_pairs={{0,8},{4,12},{8,0},{12,4},{16,24},{20,28},{24,16},{28,20},{32,40},... | collective-permute-start | bytes 196616 | tf_op jit(solution)/shard_map/ppermute | solution.py:20
  596.6 19.7 %collective-permute-start.46 = (f32[64,256]{1,0:T(8,128)S(1)}, f32[64,256]{1,0:T(8,128)S(1)}, u32[]{:S(2)}, u32[]{:S(2)}) collective-permute-start(f32[64,256]{1,0:T(8,128)S(1)} %slice.2497), channel_id=1, source_target_pairs={{0,16},{4,20},{8,24},{12,28},{16,0},{20,4},{24,8},{28,12},{32,48},... | collective-permute-start | bytes 196616 | tf_op jit(solution)/shard_map/ppermute | solution.py:20
  607.0 16.2 %collective-permute-start.52 = (f32[64,256]{1,0:T(8,128)S(1)}, f32[64,256]{1,0:T(8,128)S(1)}, u32[]{:S(2)}, u32[]{:S(2)}) collective-permute-start(f32[64,256]{1,0:T(8,128)S(1)} %slice.2511), channel_id=1, source_target_pairs={{0,32},{4,36},{8,40},{12,44},{16,48},{20,52},{24,56},{28,60},{32,0... | collective-permute-start | bytes 196616 | tf_op jit(solution)/shard_map/ppermute | solution.py:20
  614.4 11.4 %collective-permute-start.42 = (f32[32,256]{1,0:T(8,128)S(1)}, f32[32,256]{1,0:T(8,128)S(1)}, u32[]{:S(2)}, u32[]{:S(2)}) collective-permute-start(f32[32,256]{1,0:T(8,128)S(1)} %slice.2487), channel_id=1, source_target_pairs={{0,4},{4,0},{8,12},{12,8},{16,20},{20,16},{24,28},{28,24},{32,36},... | collective-permute-start | bytes 98312 | tf_op jit(solution)/shard_map/ppermute | solution.py:20
  (173 other events, 604.5 us)
